TPU v7x, 32 devices: a whole 2x2x4 slice. The times are simulated.
32 devices in a mesh: groups: 2 (over y), det: 4 (over z), blk: 2 (over x), sub: 2 (over core).
Axes of the slice: x: 2, y: 2, z: 4, core: 2. Of those that a mesh axis runs over, the one named last changes fastest.
Arguments:
- tod: float32 [256, 4, 1024], P(('groups', 'det'), None, ('blk', 'sub')), parts along dimension 0, may hold values from -30 to 30
- pixels: int32 [256, 4, 1024], P('groups', 'det', ('blk', 'sub')), parts along dimension 0, may hold values from 0 to 3071
- span_block: int32 [8, 8], P('groups', ('blk', 'sub')), parts along dimension 0, may hold values from 0 to 7
- weight_class: int32 [256], P('groups'), parts along dimension 0, may hold values from 0 to 7
- class_weight: float32 [16], P('groups'), parts along dimension 0, may hold values from 0.25 to 4
Outputs:
- signal_sum: float32 [16, 3072], P(('groups', 'blk'), ('det', 'sub')), parts along dimension 0
- weight_sum: float32 [16, 3072], P(('groups', 'blk'), ('det', 'sub')), parts along dimension 0
- hit_count: float32 [16, 3072], P(('groups', 'blk'), ('det', 'sub')), parts along dimension 0
There are 2 independent parts, one for each index of `groups`. A program takes and returns all parts, laid end to end along the dimension named above; each array names one. Nothing has to cross between parts.
All inputs are finite; a program needn't handle non-finite values.
Results may differ from a plain program's by a relative error of at most 0.005.
Values sent between devices are 32-bit elements; how exact they have to be, the bound alone decides.
No kernel may reach another device: no remote copies, remote signals or barrier semaphores. Data moves between devices by JAX's collectives and lax.ppermute only.
A program may use at most 64 MiB of HBM per device.

v0:
```python
import jax
import jax.numpy as jnp
from jax import lax
from jax.sharding import PartitionSpec as P

BLOCK_PIX = 3072
SPAN = 128
BLK_OWN = 4


def on_device(tod, pixels, span_block, weight_class, class_weight):
    classes = class_weight.shape[0]
    picker = (weight_class[:, None] == jnp.arange(classes, dtype=jnp.int32)[None, :]).astype(
        jnp.float32
    )
    weight = jnp.sum(picker * class_weight[None, :], axis=1)
    total = jnp.sum(weight)
    regrouped = lax.all_to_all(tod, "det", split_axis=1, concat_axis=0, tiled=True)
    common = jnp.sum(weight[:, None, None] * regrouped, axis=0, keepdims=True) / total
    values = (weight[:, None, None] * (regrouped - common)).astype(jnp.bfloat16)
    detectors = values.shape[0]
    samples = values.shape[2]
    spans = samples // SPAN
    groups = 4
    size_group = detectors // groups
    turns = groups * spans
    own_row = lax.dynamic_slice_in_dim(span_block, lax.axis_index("det"), 1, 0)[0]
    values = (
        values.reshape(groups, size_group, spans, SPAN)
        .transpose(0, 2, 1, 3)
        .reshape(turns, size_group, SPAN)
    )
    where = (
        pixels.reshape(groups, size_group, spans, SPAN)
        .transpose(0, 2, 1, 3)
        .reshape(turns, size_group, SPAN)
    )
    weight_low = weight.astype(jnp.bfloat16).reshape(groups, 1, size_group)
    weight_low = jnp.broadcast_to(weight_low, (groups, spans, size_group)).reshape(
        turns, size_group
    )
    span_of = jnp.broadcast_to(
        jnp.arange(spans, dtype=jnp.int32)[None, :], (groups, spans)
    ).reshape(turns)
    lanes = 128
    upper = BLOCK_PIX // lanes
    nblocks = BLK_OWN * lax.axis_size("blk")
    count = size_group * SPAN
    selector = (span_of[:, None] == jnp.arange(spans, dtype=jnp.int32)[None, :]).astype(jnp.float32)

    def bin_tile(total_map, item):
        tile_values, tile_pixels, tile_weight, select = item
        high = tile_pixels // lanes
        low = tile_pixels % lanes
        high_hot = (high[..., None] == jnp.arange(upper, dtype=jnp.int32)).astype(jnp.bfloat16)
        first = tile_values[..., None] * high_hot
        second = tile_weight[:, None, None] * high_hot
        stacked = jnp.concatenate([first, second, high_hot], axis=-1).reshape(count, 3 * upper)
        low_hot = (
            (low[..., None] == jnp.arange(lanes, dtype=jnp.int32))
            .astype(jnp.bfloat16)
            .reshape(count, lanes)
        )
        binned = lax.dot_general(
            stacked, low_hot, (((0,), (0,)), ((), ())), preferred_element_type=jnp.float32
        )
        return (total_map + select[:, None, None] * binned[None], None)

    start = jnp.zeros((spans, 3 * upper, lanes), jnp.float32)
    binned_map, unused = lax.scan(bin_tile, start, (values, where, weight_low, selector))
    binned_map = binned_map.reshape(spans, 3, BLOCK_PIX)
    count_det = lax.axis_size("det")
    count_sub = lax.axis_size("sub")
    peers = count_det * count_sub
    width = BLOCK_PIX // peers
    pieces = binned_map.reshape(spans, 3, peers, width)
    labels = jnp.broadcast_to(
        own_row.astype(jnp.float32)[:, None, None, None], (spans, 1, peers, 1)
    )
    received, got_labels = (
        lax.all_to_all(pieces, ("det", "sub"), split_axis=2, concat_axis=0, tiled=True),
        lax.all_to_all(labels, ("det", "sub"), split_axis=2, concat_axis=0, tiled=True),
    )
    received = received.reshape(peers * spans, 3 * width)
    got_labels = got_labels.reshape(peers * spans)
    placing = (got_labels[:, None] == jnp.arange(nblocks, dtype=jnp.float32)[None, :]).astype(
        jnp.float32
    )
    gathered = lax.dot_general(
        placing,
        received,
        (((0,), (0,)), ((), ())),
        precision=lax.Precision.HIGHEST,
        preferred_element_type=jnp.float32,
    )
    gathered = gathered.reshape(nblocks, 3, width)
    mine = lax.psum_scatter(gathered, "blk", scatter_dimension=0, tiled=True)
    signal_sum, weight_sum, hit_count = (mine[:, 0], mine[:, 1], mine[:, 2])
    return (signal_sum, weight_sum, hit_count)


def solution(mesh):
    placed = (
        P(("groups", "det"), None, ("blk", "sub")),
        P("groups", "det", ("blk", "sub")),
        P("groups", ("blk", "sub")),
        P("groups"),
        P("groups"),
    )
    return jax.shard_map(
        on_device,
        mesh=mesh,
        in_specs=placed,
        out_specs=(
            P(("groups", "blk"), ("det", "sub")),
            P(("groups", "blk"), ("det", "sub")),
            P(("groups", "blk"), ("det", "sub")),
        ),
        check_vma=False,
    )
```

profile of v0, /device:TPU:0, one launch (start us, length us, event | category | flops | bytes accessed | tf_op | source)
XLA Modules:
  0.0 50.1 jit_solution(9082960590155810975)
XLA Ops:
  0.6 1.6 %copy.35 = f32[32,4,256]{2,0,1:T(8,128)} copy(f32[32,4,256]{2,1,0:T(4,128)} %param.7) | data formatting | bytes 262144 | tf_op args[0]
  2.2 6.5 %all-to-all-start.1 = ((f32[32,4,256]{2,0,1:T(8,128)}), f32[32,4,256]{2,0,1:T(8,128)S(1)}, u32[]{:S(2)}, u32[]{:S(2)}) async-start(f32[32,4,256]{2,0,1:T(8,128)} %copy.35), calls=%async_computation.1 | async-start | bytes 262144 | tf_op jit(solution)/shard_map/all_to_all | solution.py:18
  8.7 0.7 %select_reduce_fusion = (f32[]{:T(128)}, f32[128]{0:T(128)S(1)}) fusion(f32[8]{0:T(128)S(1)} %copy-done.2, s32[128]{0:T(128)S(1)} %copy-done.3), kind=kLoop, calls=%fused_computation.40 | loop fusion | flops 3967 | bytes 1060 | tf_op jit(solution)/shard_map/reduce_sum | solution.py:17
  9.6 0.2 convert_reduce_fusion
  9.8 4.9 %all-to-all-done.1 = f32[32,4,256]{2,0,1:T(8,128)S(1)} async-done(((f32[32,4,256]{2,0,1:T(8,128)}), f32[32,4,256]{2,0,1:T(8,128)S(1)}, u32[]{:S(2)}, u32[]{:S(2)}) %all-to-all-start.1) | async-done | bytes 131104 | tf_op jit(solution)/shard_map/all_to_all | solution.py:18
  14.8 0.6 %broadcast_in_dim.8 = f32[2,1,8,1]{0,3,1,2:T(1,128)} broadcast(f32[2]{0:T(128)S(1)} %convert_reduce_fusion), dimensions={0} | broadcast | bytes 72 | tf_op jit(solution)/shard_map/broadcast_in_dim | solution.py:77
  15.3 3.3 %all-to-all-start = ((f32[2,1,8,1]{0,3,1,2:T(1,128)}), f32[2,1,8,1]{0,3,1,2:T(1,128)S(1)}, u32[]{:S(2)}, u32[]{:S(2)}) async-start(f32[2,1,8,1]{0,3,1,2:T(1,128)} %broadcast_in_dim.8), calls=%async_computation | async-start | bytes 8192 | tf_op jit(solution)/shard_map/all_to_all | solution.py:82
  18.8 0.7 %divide_bitcast_fusion = f32[2,128]{1,0:T(2,128)S(1)} fusion(f32[256]{0:T(256)S(1)} %fusion.17, f32[]{:T(128)} %get-tuple-element.105), kind=kLoop, calls=%fused_computation.48 | loop fusion | flops 256 | bytes 2052 | tf_op jit(solution)/shard_map/div | solution.py:19
  19.5 0.2 fusion.21
  19.7 9.3 %while.13 = (s32[]{:T(128)}, f32[2,72,128]{2,1,0:T(8,128)S(1)}, f32[8,2]{1,0:T(8,128)S(1)}, s32[8,32,128]{2,1,0:T(8,128)S(1)}, bf16[8,32,128]{2,1,0:T(8,128)(2,1...) while((s32[]{:T(128)}, f32[2,72,128]{2,1,0:T(8,128)S(1)}, f32[8,2]{1,0:T(8,128)S(1)}, ...), condition=%wide.region_4.5_spmd.clone, body=%wide.region_3.4_spmd.clone.sunk | while | flops 78440448 | bytes 1548619 | solution.py:70
  20.0 0.8 %fusion.36 = f32[72,128]{1,0:T(8,128)S(1)} fusion(s32[32,128]{1,0:T(8,128)S(1)} %add_select_fusion.5, bf16[32,128,24]{1,2,0:T(8,128)(2,1)S(1)} %fusion.33, bf16[32,128,24]{1,2,0:T(8,128)(2,1)S(1)} %get-tuple-element.169, bf16[32,128,24]{1,2,0:T(8,128)(2,1)S(1)} %get-tuple-element.170), kind=kOutput, calls=%fused_computation.2.clone.1 | convolution fusion | flops 77791232 | bytes 643072 | tf_op jit(solution)/shard_map/while/body/eval_jaxpr/dot_general | solution.py:64
  21.2 0.8 %fusion.36 = f32[72,128]{1,0:T(8,128)S(1)} fusion(s32[32,128]{1,0:T(8,128)S(1)} %add_select_fusion.5, bf16[32,128,24]{1,2,0:T(8,128)(2,1)S(1)} %fusion.33, bf16[32,128,24]{1,2,0:T(8,128)(2,1)S(1)} %get-tuple-element.169, bf16[32,128,24]{1,2,0:T(8,128)(2,1)S(1)} %get-tuple-element.170), kind=kOutput, calls=%fused_computation.2.clone.1 | convolution fusion | flops 77791232 | bytes 643072 | tf_op jit(solution)/shard_map/while/body/eval_jaxpr/dot_general | solution.py:64
  22.3 0.8 %fusion.36 = f32[72,128]{1,0:T(8,128)S(1)} fusion(s32[32,128]{1,0:T(8,128)S(1)} %add_select_fusion.5, bf16[32,128,24]{1,2,0:T(8,128)(2,1)S(1)} %fusion.33, bf16[32,128,24]{1,2,0:T(8,128)(2,1)S(1)} %get-tuple-element.169, bf16[32,128,24]{1,2,0:T(8,128)(2,1)S(1)} %get-tuple-element.170), kind=kOutput, calls=%fused_computation.2.clone.1 | convolution fusion | flops 77791232 | bytes 643072 | tf_op jit(solution)/shard_map/while/body/eval_jaxpr/dot_general | solution.py:64
  23.5 0.8 %fusion.36 = f32[72,128]{1,0:T(8,128)S(1)} fusion(s32[32,128]{1,0:T(8,128)S(1)} %add_select_fusion.5, bf16[32,128,24]{1,2,0:T(8,128)(2,1)S(1)} %fusion.33, bf16[32,128,24]{1,2,0:T(8,128)(2,1)S(1)} %get-tuple-element.169, bf16[32,128,24]{1,2,0:T(8,128)(2,1)S(1)} %get-tuple-element.170), kind=kOutput, calls=%fused_computation.2.clone.1 | convolution fusion | flops 77791232 | bytes 643072 | tf_op jit(solution)/shard_map/while/body/eval_jaxpr/dot_general | solution.py:64
  24.6 0.8 %fusion.36 = f32[72,128]{1,0:T(8,128)S(1)} fusion(s32[32,128]{1,0:T(8,128)S(1)} %add_select_fusion.5, bf16[32,128,24]{1,2,0:T(8,128)(2,1)S(1)} %fusion.33, bf16[32,128,24]{1,2,0:T(8,128)(2,1)S(1)} %get-tuple-element.169, bf16[32,128,24]{1,2,0:T(8,128)(2,1)S(1)} %get-tuple-element.170), kind=kOutput, calls=%fused_computation.2.clone.1 | convolution fusion | flops 77791232 | bytes 643072 | tf_op jit(solution)/shard_map/while/body/eval_jaxpr/dot_general | solution.py:64
  25.8 0.8 %fusion.36 = f32[72,128]{1,0:T(8,128)S(1)} fusion(s32[32,128]{1,0:T(8,128)S(1)} %add_select_fusion.5, bf16[32,128,24]{1,2,0:T(8,128)(2,1)S(1)} %fusion.33, bf16[32,128,24]{1,2,0:T(8,128)(2,1)S(1)} %get-tuple-element.169, bf16[32,128,24]{1,2,0:T(8,128)(2,1)S(1)} %get-tuple-element.170), kind=kOutput, calls=%fused_computation.2.clone.1 | convolution fusion | flops 77791232 | bytes 643072 | tf_op jit(solution)/shard_map/while/body/eval_jaxpr/dot_general | solution.py:64
  26.9 0.8 %fusion.36 = f32[72,128]{1,0:T(8,128)S(1)} fusion(s32[32,128]{1,0:T(8,128)S(1)} %add_select_fusion.5, bf16[32,128,24]{1,2,0:T(8,128)(2,1)S(1)} %fusion.33, bf16[32,128,24]{1,2,0:T(8,128)(2,1)S(1)} %get-tuple-element.169, bf16[32,128,24]{1,2,0:T(8,128)(2,1)S(1)} %get-tuple-element.170), kind=kOutput, calls=%fused_computation.2.clone.1 | convolution fusion | flops 77791232 | bytes 643072 | tf_op jit(solution)/shard_map/while/body/eval_jaxpr/dot_general | solution.py:64
  28.1 0.8 %fusion.36 = f32[72,128]{1,0:T(8,128)S(1)} fusion(s32[32,128]{1,0:T(8,128)S(1)} %add_select_fusion.5, bf16[32,128,24]{1,2,0:T(8,128)(2,1)S(1)} %fusion.33, bf16[32,128,24]{1,2,0:T(8,128)(2,1)S(1)} %get-tuple-element.169, bf16[32,128,24]{1,2,0:T(8,128)(2,1)S(1)} %get-tuple-element.170), kind=kOutput, calls=%fused_computation.2.clone.1 | convolution fusion | flops 77791232 | bytes 643072 | tf_op jit(solution)/shard_map/while/body/eval_jaxpr/dot_general | solution.py:64
  29.0 0.7 %copy.37 = f32[2,3,8,384]{3,0,1,2:T(2,128)} copy(f32[2,3,8,384]{3,2,1,0:T(8,128)S(1)} %reshape_reshape.3) | data formatting | bytes 147456 | tf_op jit(solution)/shard_map/reshape;reshape | solution.py:76
  29.7 5.0 %all-to-all-start.2 = ((f32[2,3,8,384]{3,0,1,2:T(2,128)}), f32[2,3,8,384]{3,0,1,2:T(2,128)S(1)}, u32[]{:S(2)}, u32[]{:S(2)}) async-start(f32[2,3,8,384]{3,0,1,2:T(2,128)} %copy.37), calls=%async_computation.2 | async-start | bytes 147456 | tf_op jit(solution)/shard_map/all_to_all | solution.py:81
  34.7 0.6 %dynamic-slice = u32[1]{0:T(128)} dynamic-slice(u32[32]{0:T(128)S(1)} %copy-done.4, u32[]{:T(128)S(6)} %add.43), dynamic_slice_sizes={1} | dynamic-slice | bytes 12
  36.2 4.5 %all-to-all-done.2 = f32[2,3,8,384]{3,0,1,2:T(2,128)S(1)} async-done(((f32[2,3,8,384]{3,0,1,2:T(2,128)}), f32[2,3,8,384]{3,0,1,2:T(2,128)S(1)}, u32[]{:S(2)}, u32[]{:S(2)}) %all-to-all-start.2) | async-done | bytes 73760 | tf_op jit(solution)/shard_map/all_to_all | solution.py:81
  40.9 8.6 %all-reduce = f32[8,3,384]{2,0,1:T(8,128)S(1)} all-reduce(f32[8,3,384]{2,0,1:T(8,128)S(1)} %fusion.18), channel_id=2, replica_groups=mesh['groups'=2,'det'=4,'blk'=2,'sub'=2] {'blk'}, use_global_device_ids=true, to_apply=%region_5.6.clone | all-reduce | flops 9216 | bytes 73728
  49.5 0.6 %dynamic-slice_bitcast_fusion.1 = (f32[4,384]{1,0:T(4,128)}, f32[4,384]{1,0:T(4,128)}, f32[4,384]{1,0:T(4,128)}) fusion(f32[8,3,384]{2,0,1:T(8,128)S(1)} %all-reduce, u32[]{:T(128)S(6)} %multiply.1, u32[]{:T(128)S(6)} %convert.1, u32[]{:T(128)S(6)} %convert), kind=kLoop, calls=%fused_computation.37 | loop fusion | bytes 36876 | tf_op jit(solution)/shard_map/squeeze | solution.py:98
  (92 shorter events, 3.3 us)
Async XLA Ops:
  2.2 6.5 %copy-start.2 = (f32[8]{0:T(128)S(1)}, f32[8]{0:T(128)}, u32[]{:S(2)}) copy-start(f32[8]{0:T(128)} %param.11) | copy-start | bytes 100
  2.2 6.5 %copy-start.3 = (s32[128]{0:T(128)S(1)}, s32[128]{0:T(128)}, u32[]{:S(2)}) copy-start(s32[128]{0:T(128)} %param.10) | copy-start | bytes 1540
  2.2 7.3 %copy-start = (s32[128,1,256]{2,1,0:T(1,128)S(1)}, s32[128,1,256]{2,1,0:T(1,128)}, u32[]{:S(2)}) copy-start(s32[128,1,256]{2,1,0:T(1,128)} %param.8) | copy-start | bytes 393220
  2.2 12.6 %all-to-all-start.1 = ((f32[32,4,256]{2,0,1:T(8,128)}), f32[32,4,256]{2,0,1:T(8,128)S(1)}, u32[]{:S(2)}, u32[]{:S(2)}) async-start(f32[32,4,256]{2,0,1:T(8,128)} %copy.35), calls=%async_computation.1 | async-start | bytes 262144 | tf_op jit(solution)/shard_map/all_to_all | solution.py:18
  8.7 0.9 %copy-start.1 = (s32[4,2]{0,1:T(2,128)S(1)}, s32[4,2]{0,1:T(2,128)}, u32[]{:S(2)}) copy-start(s32[4,2]{0,1:T(2,128)} %param.9) | copy-start | bytes 100
  15.3 14.3 %all-to-all-start = ((f32[2,1,8,1]{0,3,1,2:T(1,128)}), f32[2,1,8,1]{0,3,1,2:T(1,128)S(1)}, u32[]{:S(2)}, u32[]{:S(2)}) async-start(f32[2,1,8,1]{0,3,1,2:T(1,128)} %broadcast_in_dim.8), calls=%async_computation | async-start | bytes 8192 | tf_op jit(solution)/shard_map/all_to_all | solution.py:82
  29.0 5.7 %copy-start.4 = (u32[32]{0:T(128)S(1)}, u32[32]{0:T(128)}, u32[]{:S(2)}) copy-start(u32[32]{0:T(128)} %constant.84) | copy-start | bytes 388
  29.7 11.0 %all-to-all-start.2 = ((f32[2,3,8,384]{3,0,1,2:T(2,128)}), f32[2,3,8,384]{3,0,1,2:T(2,128)S(1)}, u32[]{:S(2)}, u32[]{:S(2)}) async-start(f32[2,3,8,384]{3,0,1,2:T(2,128)} %copy.37), calls=%async_computation.2 | async-start | bytes 147456 | tf_op jit(solution)/shard_map/all_to_all | solution.py:81
where the time goes:
time: 50.5 us; the launch traced here: 50.1 us
  starting transfers between devices  14.8 us (29%)
  waiting for transfers between devices  9.42 us (19%)
  blocking collectives  8.57 us (17%)
  matrix products  6.57 us (13%)
  local copies, waits for them, and re-layouts  4.85 us (10%)
  other arithmetic  4.02 us (8%)
  between operations  1.39 us (3%)
    unnamed x1, blocking collectives  8.57 us
    all_to_all x1, starting transfers between devices, on_device(): lax.all_to_all(tod, 'det', split_axis=1, concat_axis=0, tiled=True)  6.48 us
    dot_general x8, matrix products, bin_tile(): lax.dot_general(stacked, low_hot, (((0,), (0,)), ((), ())), preferred_ele...  6.42 us
    all_to_all x1, starting transfers between devices, on_device(): lax.all_to_all(pieces, ('det', 'sub'), split_axis=2, concat_axis=0, tiled...  5.03 us
    all_to_all x1, waiting for transfers between devices, on_device(): lax.all_to_all(tod, 'det', split_axis=1, concat_axis=0, tiled=True)  4.93 us
    all_to_all x1, waiting for transfers between devices, on_device(): lax.all_to_all(pieces, ('det', 'sub'), split_axis=2, concat_axis=0, tiled...  4.49 us
    all_to_all x1, starting transfers between devices, on_device(): lax.all_to_all(labels, ('det', 'sub'), split_axis=2, concat_axis=0, tiled...  3.31 us
    unnamed x12, local copies, waits for them, and re-layouts  2.17 us
  transfers between devices with their start and end apart: 3, of which 2 were waited for; matrix products, arithmetic and copies ran while one was open for 25% of the time, Pallas kernels for 0%

commit v1 on v0

--- a/solution.py
+++ b/solution.py
@@ -78,7 +78,15 @@
         own_row.astype(jnp.float32)[:, None, None, None], (spans, 1, peers, 1)
     )
     received, got_labels = (
-        lax.all_to_all(pieces, ("det", "sub"), split_axis=2, concat_axis=0, tiled=True),
+        jnp.concatenate(
+            lax.all_to_all(
+                jnp.stack(jnp.split(pieces, lax.axis_size(("det", "sub")), axis=2)),
+                ("det", "sub"),
+                0,
+                0,
+            ),
+            axis=0,
+        ),
         lax.all_to_all(labels, ("det", "sub"), split_axis=2, concat_axis=0, tiled=True),
     )
     received = received.reshape(peers * spans, 3 * width)

time: 50.5 us -> 54.8 us (1.085)
  local copies, waits for them, and re-layouts: 4.85 us -> 8.97 us
    unnamed x12 -> x19, local copies, waits for them, and re-layouts: 2.17 us -> 6.38 us
    another operation x2 -> x1, local copies, waits for them, and re-layouts: 0.68 us -> 0.02 us  [on_device(): pieces = binned_map.reshape(spans, 3, peers, width)]
    another operation x0 -> x1, local copies, waits for them, and re-layouts: none -> 0.6 us  [on_device(): jnp.stack(jnp.split(pieces, lax.axis_size(('det', 'sub')), axis=2))]
  transfers between devices with their start and end apart: 3 -> 3, of which waited for: 2 -> 2; matrix products, arithmetic and copies ran while one was open for 25% -> 30% of each run, Pallas kernels for 0% -> 0%
where the time goes in v1:
time: 54.8 us; the launch traced here: 54.4 us
  starting transfers between devices  14.8 us (27%)
  waiting for transfers between devices  9.42 us (17%)
  local copies, waits for them, and re-layouts  8.97 us (16%)
  blocking collectives  8.59 us (16%)
  matrix products  6.57 us (12%)
  other arithmetic  4.21 us (8%)
  between operations  1.39 us (3%)
    unnamed x1, blocking collectives  8.59 us
    all_to_all x1, starting transfers between devices, on_device(): lax.all_to_all(tod, 'det', split_axis=1, concat_axis=0, tiled=True)  6.48 us
    dot_general x8, matrix products, bin_tile(): lax.dot_general(stacked, low_hot, (((0,), (0,)), ((), ())), preferred_ele...  6.42 us
    unnamed x19, local copies, waits for them, and re-layouts  6.38 us
    all_to_all x1, starting transfers between devices, on_device(): lax.all_to_all(jnp.stack(jnp.split(pieces, lax.axis_size(('det', 'sub')),...  5.03 us
    all_to_all x1, waiting for transfers between devices, on_device(): lax.all_to_all(tod, 'det', split_axis=1, concat_axis=0, tiled=True)  4.93 us
    all_to_all x1, waiting for transfers between devices, on_device(): lax.all_to_all(jnp.stack(jnp.split(pieces, lax.axis_size(('det', 'sub')),...  4.49 us
    all_to_all x1, starting transfers between devices, on_device(): lax.all_to_all(labels, ('det', 'sub'), split_axis=2, concat_axis=0, tiled...  3.31 us
  transfers between devices with their start and end apart: 3, of which 2 were waited for; matrix products, arithmetic and copies ran while one was open for 30% of the time, Pallas kernels for 0%

profile of v1, /device:TPU:0, one launch (start us, length us, event | category | flops | bytes accessed | tf_op | source)
XLA Modules:
  0.0 54.4 jit_solution(8419422077658927663)
XLA Ops:
  0.6 1.6 %copy.25 = f32[32,4,256]{2,0,1:T(8,128)} copy(f32[32,4,256]{2,1,0:T(4,128)} %param.7) | data formatting | bytes 262144 | tf_op args[0]
  2.2 6.5 %all-to-all-start.1 = ((f32[32,4,256]{2,0,1:T(8,128)}), f32[32,4,256]{2,0,1:T(8,128)S(1)}, u32[]{:S(2)}, u32[]{:S(2)}) async-start(f32[32,4,256]{2,0,1:T(8,128)} %copy.25), calls=%async_computation.1 | async-start | bytes 262144 | tf_op jit(solution)/shard_map/all_to_all | solution.py:18
  8.7 0.7 %select_reduce_fusion = (f32[]{:T(128)}, f32[128]{0:T(128)S(1)}) fusion(f32[8]{0:T(128)S(1)} %copy-done.2, s32[128]{0:T(128)S(1)} %copy-done.3), kind=kLoop, calls=%fused_computation.56 | loop fusion | flops 3967 | bytes 1060 | tf_op jit(solution)/shard_map/reduce_sum | solution.py:17
  9.8 4.9 %all-to-all-done.1 = f32[32,4,256]{2,0,1:T(8,128)S(1)} async-done(((f32[32,4,256]{2,0,1:T(8,128)}), f32[32,4,256]{2,0,1:T(8,128)S(1)}, u32[]{:S(2)}, u32[]{:S(2)}) %all-to-all-start.1) | async-done | bytes 131104 | tf_op jit(solution)/shard_map/all_to_all | solution.py:18
  15.4 3.3 %all-to-all-start = ((f32[2,1,8,1]{0,3,1,2:T(1,128)}), f32[2,1,8,1]{0,3,1,2:T(1,128)S(1)}, u32[]{:S(2)}, u32[]{:S(2)}) async-start(f32[2,1,8,1]{0,3,1,2:T(1,128)} %broadcast_in_dim.8), calls=%async_computation | async-start | bytes 8192 | tf_op jit(solution)/shard_map/all_to_all | solution.py:90
  18.8 0.7 %divide_bitcast_fusion = f32[2,128]{1,0:T(2,128)S(1)} fusion(f32[256]{0:T(256)S(1)} %fusion.17, f32[]{:T(128)} %get-tuple-element.105), kind=kLoop, calls=%fused_computation.64 | loop fusion | flops 256 | bytes 2052 | tf_op jit(solution)/shard_map/div | solution.py:19
  19.7 9.2 %while.13 = (s32[]{:T(128)}, f32[2,72,128]{2,1,0:T(8,128)S(1)}, f32[8,2]{1,0:T(8,128)S(1)}, s32[8,32,128]{2,1,0:T(8,128)S(1)}, bf16[8,32,128]{2,1,0:T(8,128)(2,1...) while((s32[]{:T(128)}, f32[2,72,128]{2,1,0:T(8,128)S(1)}, f32[8,2]{1,0:T(8,128)S(1)}, ...), condition=%wide.region_4.5_spmd.clone, body=%wide.region_3.4_spmd.clone.sunk | while | flops 78440448 | bytes 1548619 | solution.py:70
  20.0 0.8 %fusion.36 = f32[72,128]{1,0:T(8,128)S(1)} fusion(s32[32,128]{1,0:T(8,128)S(1)} %add_select_fusion.5, bf16[32,128,24]{1,2,0:T(8,128)(2,1)S(1)} %fusion.33, bf16[32,128,24]{1,2,0:T(8,128)(2,1)S(1)} %get-tuple-element.169, bf16[32,128,24]{1,2,0:T(8,128)(2,1)S(1)} %get-tuple-element.170), kind=kOutput, calls=%fused_computation.2.clone.1 | convolution fusion | flops 77791232 | bytes 643072 | tf_op jit(solution)/shard_map/while/body/eval_jaxpr/dot_general | solution.py:64
  21.2 0.8 %fusion.36 = f32[72,128]{1,0:T(8,128)S(1)} fusion(s32[32,128]{1,0:T(8,128)S(1)} %add_select_fusion.5, bf16[32,128,24]{1,2,0:T(8,128)(2,1)S(1)} %fusion.33, bf16[32,128,24]{1,2,0:T(8,128)(2,1)S(1)} %get-tuple-element.169, bf16[32,128,24]{1,2,0:T(8,128)(2,1)S(1)} %get-tuple-element.170), kind=kOutput, calls=%fused_computation.2.clone.1 | convolution fusion | flops 77791232 | bytes 643072 | tf_op jit(solution)/shard_map/while/body/eval_jaxpr/dot_general | solution.py:64
  22.3 0.8 %fusion.36 = f32[72,128]{1,0:T(8,128)S(1)} fusion(s32[32,128]{1,0:T(8,128)S(1)} %add_select_fusion.5, bf16[32,128,24]{1,2,0:T(8,128)(2,1)S(1)} %fusion.33, bf16[32,128,24]{1,2,0:T(8,128)(2,1)S(1)} %get-tuple-element.169, bf16[32,128,24]{1,2,0:T(8,128)(2,1)S(1)} %get-tuple-element.170), kind=kOutput, calls=%fused_computation.2.clone.1 | convolution fusion | flops 77791232 | bytes 643072 | tf_op jit(solution)/shard_map/while/body/eval_jaxpr/dot_general | solution.py:64
  23.5 0.8 %fusion.36 = f32[72,128]{1,0:T(8,128)S(1)} fusion(s32[32,128]{1,0:T(8,128)S(1)} %add_select_fusion.5, bf16[32,128,24]{1,2,0:T(8,128)(2,1)S(1)} %fusion.33, bf16[32,128,24]{1,2,0:T(8,128)(2,1)S(1)} %get-tuple-element.169, bf16[32,128,24]{1,2,0:T(8,128)(2,1)S(1)} %get-tuple-element.170), kind=kOutput, calls=%fused_computation.2.clone.1 | convolution fusion | flops 77791232 | bytes 643072 | tf_op jit(solution)/shard_map/while/body/eval_jaxpr/dot_general | solution.py:64
  24.6 0.8 %fusion.36 = f32[72,128]{1,0:T(8,128)S(1)} fusion(s32[32,128]{1,0:T(8,128)S(1)} %add_select_fusion.5, bf16[32,128,24]{1,2,0:T(8,128)(2,1)S(1)} %fusion.33, bf16[32,128,24]{1,2,0:T(8,128)(2,1)S(1)} %get-tuple-element.169, bf16[32,128,24]{1,2,0:T(8,128)(2,1)S(1)} %get-tuple-element.170), kind=kOutput, calls=%fused_computation.2.clone.1 | convolution fusion | flops 77791232 | bytes 643072 | tf_op jit(solution)/shard_map/while/body/eval_jaxpr/dot_general | solution.py:64
  25.8 0.8 %fusion.36 = f32[72,128]{1,0:T(8,128)S(1)} fusion(s32[32,128]{1,0:T(8,128)S(1)} %add_select_fusion.5, bf16[32,128,24]{1,2,0:T(8,128)(2,1)S(1)} %fusion.33, bf16[32,128,24]{1,2,0:T(8,128)(2,1)S(1)} %get-tuple-element.169, bf16[32,128,24]{1,2,0:T(8,128)(2,1)S(1)} %get-tuple-element.170), kind=kOutput, calls=%fused_computation.2.clone.1 | convolution fusion | flops 77791232 | bytes 643072 | tf_op jit(solution)/shard_map/while/body/eval_jaxpr/dot_general | solution.py:64
  26.9 0.8 %fusion.36 = f32[72,128]{1,0:T(8,128)S(1)} fusion(s32[32,128]{1,0:T(8,128)S(1)} %add_select_fusion.5, bf16[32,128,24]{1,2,0:T(8,128)(2,1)S(1)} %fusion.33, bf16[32,128,24]{1,2,0:T(8,128)(2,1)S(1)} %get-tuple-element.169, bf16[32,128,24]{1,2,0:T(8,128)(2,1)S(1)} %get-tuple-element.170), kind=kOutput, calls=%fused_computation.2.clone.1 | convolution fusion | flops 77791232 | bytes 643072 | tf_op jit(solution)/shard_map/while/body/eval_jaxpr/dot_general | solution.py:64
  28.1 0.8 %fusion.36 = f32[72,128]{1,0:T(8,128)S(1)} fusion(s32[32,128]{1,0:T(8,128)S(1)} %add_select_fusion.5, bf16[32,128,24]{1,2,0:T(8,128)(2,1)S(1)} %fusion.33, bf16[32,128,24]{1,2,0:T(8,128)(2,1)S(1)} %get-tuple-element.169, bf16[32,128,24]{1,2,0:T(8,128)(2,1)S(1)} %get-tuple-element.170), kind=kOutput, calls=%fused_computation.2.clone.1 | convolution fusion | flops 77791232 | bytes 643072 | tf_op jit(solution)/shard_map/while/body/eval_jaxpr/dot_general | solution.py:64
  30.8 0.6 %constant_dynamic-update-slice_fusion.4 = f32[8,2,3,1,384]{4,3,2,1,0:T(1,128)} fusion(f32[8,2,3,1,384]{4,3,2,1,0:T(1,128)} %constant_dynamic-update-slice_fusion.5, f32[2,3,8,384]{3,2,1,0:T(8,128)S(1)} %reshape_reshape.6), kind=kLoop, calls=%fused_computation.41 | loop fusion | bytes 18432
  31.4 0.6 %constant_dynamic-update-slice_fusion.3 = f32[8,2,3,1,384]{4,3,2,1,0:T(1,128)} fusion(f32[8,2,3,1,384]{4,3,2,1,0:T(1,128)} %constant_dynamic-update-slice_fusion.4, f32[2,3,8,384]{3,2,1,0:T(8,128)S(1)} %reshape_reshape.6), kind=kLoop, calls=%fused_computation.40 | loop fusion | bytes 18432
  32.0 0.6 %constant_dynamic-update-slice_fusion.2 = f32[8,2,3,1,384]{4,3,2,1,0:T(1,128)} fusion(f32[8,2,3,1,384]{4,3,2,1,0:T(1,128)} %constant_dynamic-update-slice_fusion.3, f32[2,3,8,384]{3,2,1,0:T(8,128)S(1)} %reshape_reshape.6), kind=kLoop, calls=%fused_computation.39 | loop fusion | bytes 18432
  32.6 0.6 %constant_dynamic-update-slice_fusion.1 = f32[8,2,3,1,384]{4,3,2,1,0:T(1,128)} fusion(f32[8,2,3,1,384]{4,3,2,1,0:T(1,128)} %constant_dynamic-update-slice_fusion.2, f32[2,3,8,384]{3,2,1,0:T(8,128)S(1)} %reshape_reshape.6), kind=kLoop, calls=%fused_computation.38 | loop fusion | bytes 18432
  33.2 0.6 %constant_dynamic-update-slice_fusion = f32[8,2,3,1,384]{4,3,2,1,0:T(1,128)} fusion(f32[8,2,3,1,384]{4,3,2,1,0:T(1,128)} %constant_dynamic-update-slice_fusion.1, f32[2,3,8,384]{3,2,1,0:T(8,128)S(1)} %reshape_reshape.6), kind=kLoop, calls=%fused_computation.37 | loop fusion | bytes 18432 | tf_op jit(solution)/shard_map/stack | solution.py:83
  33.8 5.0 %all-to-all-start.2 = ((f32[8,2,3,1,384]{4,3,2,1,0:T(1,128)}), f32[8,2,3,1,384]{4,3,2,1,0:T(1,128)S(1)}, u32[]{:S(2)}, u32[]{:S(2)}) async-start(f32[8,2,3,1,384]{4,3,2,1,0:T(1,128)} %constant_dynamic-update-slice_fusion), calls=%async_computation.2 | async-start | bytes 147456 | tf_op jit(solution)/shard_map/all_to_all | solution.py:82
  40.4 4.5 %all-to-all-done.2 = f32[8,2,3,1,384]{4,3,2,1,0:T(1,128)S(1)} async-done(((f32[8,2,3,1,384]{4,3,2,1,0:T(1,128)}), f32[8,2,3,1,384]{4,3,2,1,0:T(1,128)S(1)}, u32[]{:S(2)}, u32[]{:S(2)}) %all-to-all-start.2) | async-done | bytes 73760 | tf_op jit(solution)/shard_map/all_to_all | solution.py:82
  45.2 8.6 %all-reduce = f32[8,3,384]{2,0,1:T(8,128)S(1)} all-reduce(f32[8,3,384]{2,0,1:T(8,128)S(1)} %fusion.18), channel_id=2, replica_groups=mesh['groups'=2,'det'=4,'blk'=2,'sub'=2] {'blk'}, use_global_device_ids=true, to_apply=%region_5.6.clone | all-reduce | flops 9216 | bytes 73728
  53.8 0.6 %dynamic-slice_bitcast_fusion.1 = (f32[4,384]{1,0:T(4,128)}, f32[4,384]{1,0:T(4,128)}, f32[4,384]{1,0:T(4,128)}) fusion(f32[8,3,384]{2,0,1:T(8,128)S(1)} %all-reduce, u32[]{:T(128)S(6)} %multiply.1, u32[]{:T(128)S(6)} %convert.1, u32[]{:T(128)S(6)} %convert), kind=kLoop, calls=%fused_computation.53 | loop fusion | bytes 36876 | tf_op jit(solution)/shard_map/squeeze | solution.py:106
  (99 shorter events, 6.8 us)
Async XLA Ops:
  2.2 6.5 %copy-start.2 = (f32[8]{0:T(128)S(1)}, f32[8]{0:T(128)}, u32[]{:S(2)}) copy-start(f32[8]{0:T(128)} %param.11) | copy-start | bytes 100
  2.2 6.5 %copy-start.3 = (s32[128]{0:T(128)S(1)}, s32[128]{0:T(128)}, u32[]{:S(2)}) copy-start(s32[128]{0:T(128)} %param.10) | copy-start | bytes 1540
  2.2 7.3 %copy-start = (s32[128,1,256]{2,1,0:T(1,128)S(1)}, s32[128,1,256]{2,1,0:T(1,128)}, u32[]{:S(2)}) copy-start(s32[128,1,256]{2,1,0:T(1,128)} %param.8) | copy-start | bytes 393220
  2.2 12.6 %all-to-all-start.1 = ((f32[32,4,256]{2,0,1:T(8,128)}), f32[32,4,256]{2,0,1:T(8,128)S(1)}, u32[]{:S(2)}, u32[]{:S(2)}) async-start(f32[32,4,256]{2,0,1:T(8,128)} %copy.25), calls=%async_computation.1 | async-start | bytes 262144 | tf_op jit(solution)/shard_map/all_to_all | solution.py:18
  8.7 0.9 %copy-start.1 = (s32[4,2]{0,1:T(2,128)S(1)}, s32[4,2]{0,1:T(2,128)}, u32[]{:S(2)}) copy-start(s32[4,2]{0,1:T(2,128)} %param.9) | copy-start | bytes 100
  15.4 18.5 %all-to-all-start = ((f32[2,1,8,1]{0,3,1,2:T(1,128)}), f32[2,1,8,1]{0,3,1,2:T(1,128)S(1)}, u32[]{:S(2)}, u32[]{:S(2)}) async-start(f32[2,1,8,1]{0,3,1,2:T(1,128)} %broadcast_in_dim.8), calls=%async_computation | async-start | bytes 8192 | tf_op jit(solution)/shard_map/all_to_all | solution.py:90
  29.0 9.9 %copy-start.4 = (u32[32]{0:T(128)S(1)}, u32[32]{0:T(128)}, u32[]{:S(2)}) copy-start(u32[32]{0:T(128)} %constant.84) | copy-start | bytes 388
  33.8 11.0 %all-to-all-start.2 = ((f32[8,2,3,1,384]{4,3,2,1,0:T(1,128)}), f32[8,2,3,1,384]{4,3,2,1,0:T(1,128)S(1)}, u32[]{:S(2)}, u32[]{:S(2)}) async-start(f32[8,2,3,1,384]{4,3,2,1,0:T(1,128)} %constant_dynamic-update-slice_fusion), calls=%async_computation.2 | async-start | bytes 147456 | tf_op jit(solution)/shard_map/all_to_all | solution.py:82
